TPU v7x, 32 devices: a whole 2x2x4 slice. The times are simulated.
32 devices in a mesh: seq: 8 (over z, y), head: 4 (over x, core).
Axes of the slice: x: 2, y: 2, z: 4, core: 2. Of those that a mesh axis runs over, the one named last changes fastest.
Arguments:
- queries: bfloat16 [2, 64, 64, 128], P(None, 'head'), may hold values from -9 to 9
- cache_keys: bfloat16 [2, 8, 8192, 128], P(None, 'head', 'seq'), may hold values from -10 to 10
- cache_values: bfloat16 [2, 8, 8192, 128], P(None, 'head', 'seq'), may hold values from -6 to 6
- new_keys: bfloat16 [2, 8, 64, 128], P(None, 'head'), may hold values from -20 to 20
- new_values: bfloat16 [2, 8, 64, 128], P(None, 'head'), may hold values from -6 to 6
- parents: int32 [2, 64], replicated, may hold values from 0 to 62, as said below
- path: int32 [2, 6], replicated, may hold values from 0 to 63, as said below
- lengths: int32 [2], replicated, may hold values from 2048 to 8192, as said below
- draft_tokens: int32 [2, 64], replicated, may hold values from 0 to 65535
- residual: bfloat16 [2, 64, 8192], P(None, None, 'seq'), may hold values from -8 to 8
- out_weight: bfloat16 [8192, 8192], P('head', 'seq'), may hold values from -0.0625 to 0.0625
- norm_gain: bfloat16 [8192], P('seq'), may hold values from 0.5 to 1.5
- vocab_weight: bfloat16 [8192, 65536], P(None, ('seq', 'head')), may hold values from -3 to 3
Outputs:
- path_logits: float32 [2, 6, 65536], P(None, None, ('seq', 'head'))
- draft_logprob: float32 [2, 64], replicated
Inputs may be any that keep to these rules, and one draw needn't show every extreme that they name: parents[b, 0] is 0; for every other node n, parents[b, n] is a smaller node number. path[b] lists 6 different nodes: node 0 first, and each later entry is a child (by parents) of the entry before it. `lengths`: at least one sequence uses all 8192 cache positions.
All inputs are finite; a program needn't handle non-finite values.
Results may differ from a plain program's by a relative error of at most 0.006.
Values may be sent and summed in bfloat16 or wider, within the bound.
A program may use at most 128 MiB of HBM per device.

v0:
```python
import jax
import jax.numpy as jnp
from jax import lax
from jax.sharding import PartitionSpec as P

D = 8192
lowest = -1e30
epsilon = 1e-05


def ancestors(parents):
    node_count = parents.shape[-1]
    node_ids = jnp.arange(node_count, dtype=jnp.int32)
    linked = (parents[..., :, None] == node_ids[None, None, :]).astype(jnp.float32)
    reached = jnp.maximum(linked, jnp.eye(node_count, dtype=jnp.float32)[None])
    for _ in range(node_count.bit_length()):
        reached = jnp.minimum(jnp.einsum("bij,bjk->bik", reached, reached), 1.0)
    return reached > 0.5


def block_state(scores, visible, values):
    masked = jnp.where(visible, scores, lowest)
    block_max = jnp.max(masked, axis=-1)
    weights = jnp.where(visible, jnp.exp(masked - block_max[..., None]), 0.0).astype(jnp.bfloat16)
    block_total = jnp.sum(weights.astype(jnp.float32), axis=-1)
    block_out = jnp.einsum("kqc,kcd->kqd", weights, values, preferred_element_type=jnp.float32)
    return (block_max, block_total, block_out)


def join_states(earlier, later):
    summit = jnp.maximum(earlier[0], later[0])
    damp_early = jnp.exp(earlier[0] - summit)
    damp_later = jnp.exp(later[0] - summit)
    total_joined = earlier[1] * damp_early + later[1] * damp_later
    out_joined = earlier[2] * damp_early[..., None] + later[2] * damp_later[..., None]
    return (summit, total_joined, out_joined)


def on_device(
    queries,
    cache_keys,
    cache_values,
    new_keys,
    new_values,
    parents,
    path,
    lengths,
    draft_tokens,
    residual,
    out_weight,
    norm_gain,
    vocab_weight,
):
    batch_size, heads_local, node_count, head_dim = queries.shape
    kv_local = cache_keys.shape[1]
    span_local = cache_keys.shape[2]
    group_size = heads_local // kv_local
    score_scale = head_dim ** (-0.5)
    seq_index = lax.axis_index("seq")
    reached = ancestors(parents)
    is_owner = seq_index == 0
    offsets = seq_index * span_local + jnp.arange(span_local, dtype=jnp.int32)

    def per_sequence(entries):
        query_block, key_block, value_block, tree_keys, tree_values, reach_row, length = entries
        grouped = query_block.reshape(kv_local, group_size * node_count, head_dim)
        scores = (
            jnp.einsum("kqd,kcd->kqc", grouped, key_block, preferred_element_type=jnp.float32)
            * score_scale
        )
        live_keys = (offsets < length)[None, None, :]
        cache_state = block_state(scores, live_keys, value_block)
        tree_scores = (
            jnp.einsum("kqd,kcd->kqc", grouped, tree_keys, preferred_element_type=jnp.float32)
            * score_scale
        )
        tree_seen = jnp.logical_and(jnp.tile(reach_row, (group_size, 1))[None], is_owner)
        tree_state = block_state(tree_scores, tree_seen, tree_values)
        return join_states(cache_state, tree_state)

    maxima, totals, outputs = lax.map(
        per_sequence, (queries, cache_keys, cache_values, new_keys, new_values, reached, lengths)
    )
    weight_heads = out_weight.reshape(heads_local, head_dim, -1)
    highest = lax.pmax(maxima, "seq")
    factors = jnp.exp(maxima - highest)
    scaled = (outputs * factors[..., None]).reshape(batch_size, heads_local, node_count, head_dim)
    summed = (totals * factors).reshape(batch_size, heads_local, node_count)
    share_out, share_total = (
        lax.psum_scatter(scaled, "seq", scatter_dimension=2, tiled=True),
        lax.psum_scatter(summed, "seq", scatter_dimension=2, tiled=True),
    )
    attention = (share_out / share_total[..., None]).astype(jnp.bfloat16)
    projected = jnp.einsum(
        "bhnd,hdc->bnc",
        lax.all_gather(attention, "seq", axis=2, tiled=True),
        weight_heads,
        preferred_element_type=jnp.float32,
    )
    vocab_local = vocab_weight.shape[1]
    projected = lax.psum(projected, "head")
    stream = residual.astype(jnp.float32) + projected
    gain_part = norm_gain.astype(jnp.float32)
    square_sum = lax.psum(jnp.sum(stream * stream, axis=-1), "seq")
    normed = (stream * lax.rsqrt(square_sum / D + epsilon)[..., None] * gain_part).astype(
        jnp.bfloat16
    )
    portion = lax.all_gather(normed, "seq", axis=2, tiled=True)
    flat_part = portion.reshape(batch_size * node_count, portion.shape[2])
    logits = jnp.dot(flat_part, vocab_weight, preferred_element_type=jnp.float32)
    logits = logits.reshape(batch_size, node_count, vocab_local)
    vocab_first = lax.axis_index(("seq", "head")) * vocab_local
    vocab_ids = jnp.arange(vocab_local, dtype=jnp.int32) + vocab_first
    picked = jnp.sum(jnp.where(draft_tokens[..., None] == vocab_ids, logits, 0.0), axis=-1)
    local_max = jnp.max(logits, axis=-1)
    vocab_top = lax.pmax(local_max, ("seq", "head"))
    local_sum = jnp.sum(jnp.exp(logits - vocab_top[..., None]), axis=-1)
    exp_sums, picked = lax.psum((local_sum, picked), ("seq", "head"))
    draft_logprob = picked - (vocab_top + jnp.log(exp_sums))
    path_logits = jnp.take_along_axis(logits, path[:, :, None], axis=1)
    return (path_logits, draft_logprob)


def solution(mesh):
    placed = (
        P(None, "head", None, None),
        P(None, "head", "seq", None),
        P(None, "head", "seq", None),
        P(None, "head", None, None),
        P(None, "head", None, None),
        P(),
        P(),
        P(),
        P(),
        P(None, None, "seq"),
        P("head", "seq"),
        P("seq"),
        P(None, ("seq", "head")),
    )
    return jax.shard_map(
        on_device,
        mesh=mesh,
        in_specs=placed,
        out_specs=(P(None, None, ("seq", "head")), P()),
        check_vma=False,
    )
```

profile of v0, /device:TPU:0, one launch (start us, length us, event | category | flops | bytes accessed | tf_op | source)
XLA Modules:
  0.0 349.0 jit_solution(16134530394701500435)
XLA Ops:
  7.2 0.0 reduce-scatter.2.cloned.1.call-start
  7.3 1.0 convolution_minimum_fusion.6
  8.2 0.3 convolution_minimum_fusion.4
  8.5 0.3 convolution_minimum_fusion.2
  8.8 0.3 fusion.30
  9.1 0.0 copy-start.6
  9.1 17.6 %while.15 = (s32[]{:T(128)}, f32[2,2,512]{2,1,0:T(2,128)S(1)}, f32[2,2,512]{2,1,0:T(2,128)S(1)}, f32[2,2,512,128]{3,2,1,0:T(8,128)S(1)}, s32[2]{0:T(128)}, /*ind...) while((s32[]{:T(128)}, f32[2,2,512]{2,1,0:T(2,128)S(1)}, ...), condition=%wide.region_5.6_spmd.clone, body=%wide.region_0.5_spmd.clone.sunk | while | flops 587279360 | bytes 21873904 | solution.py:81
  9.1 1.0 constant_dynamic-slice_fusion.5
  10.1 0.1 copy.30
  10.3 0.2 and.42
  10.4 1.0 fusion.69
  11.4 0.1 convert_reduce_fusion.4
  11.5 1.2 dynamic_slice.68
  12.7 0.6 add_compare_fusion.2
  13.3 0.0 copy-start.1
  13.3 0.0 copy-start.5
  13.3 2.0 fusion.70
  15.3 1.2 convert_reduce_fusion.5
  16.5 0.3 convolution_multiply_fusion.4
  16.9 1.1 fusion.73
  17.9 1.0 constant_dynamic-slice_fusion.5
  18.9 0.1 copy.30
  19.1 0.2 and.42
  19.2 1.0 fusion.69
  20.2 0.1 convert_reduce_fusion.4
  20.3 1.2 dynamic_slice.68
  21.5 0.6 add_compare_fusion.2
  22.1 0.0 copy-start.1
  22.1 0.0 copy-start.5
  22.1 2.0 fusion.70
  24.1 1.2 convert_reduce_fusion.5
  25.3 0.3 convolution_multiply_fusion.4
  25.7 1.1 fusion.73
  26.7 23.4 %pmax.14 = f32[2,2,512]{2,1,0:T(2,128)S(1)} all-reduce(f32[2,2,512]{2,1,0:T(2,128)S(1)} %get-tuple-element.72), channel_id=1, replica_groups=mesh['seq'=8,'head'=4] {'seq'}, use_global_device_ids=true, to_apply=%region_6.7 | all-reduce | flops 2048 | bytes 16384 | tf_op jit(solution)/shard_map/pmax | solution.py:85
  50.2 1.3 broadcast_multiply_fusion
  51.5 0.0 reduce-scatter.2.cloned.1.call-update
  51.5 0.0 all-reduce.4.cloned.1.call-start
  51.6 0.1 reshape.133
  51.7 0.1 copy.24
  51.8 0.6 dynamic-slice
  53.0 33.4 %all-reduce = f32[2,16,64]{1,0,2:T(2,128)S(1)} all-reduce(f32[2,16,64]{1,0,2:T(2,128)S(1)} %copy.24), channel_id=3, replica_groups=mesh['seq'=8,'head'=4] {'seq'}, use_global_device_ids=true, to_apply=%region_8.9.clone | all-reduce | flops 2048 | bytes 16384
  86.4 0.0 copy-start.2
  86.5 0.1 copy.25
  86.6 27.2 %reduce-scatter.2.cloned.1.call-done = f32[2,16,8,128]{3,2,1,0:T(8,128)} async-done(((f32[2,16,64,128]{3,2,1,0:T(8,128)}), f32[2,16,8,128]{3,2,1,0:T(8,128)}) %reduce-scatter.2.cloned.1.call-update) | async-done | bytes 131088 | tf_op jit(solution)/shard_map/reduce_scatter | solution.py:90
  113.7 1.0 divide_convert_fusion
  114.7 27.1 %all_gather.6 = bf16[2,16,64,128]{3,2,1,0:T(8,128)(2,1)S(1)} all-gather(bf16[2,16,8,128]{3,2,1,0:T(8,128)(2,1)S(1)} %divide_convert_fusion), channel_id=1, replica_groups=mesh['seq'=8,'head'=4] {'seq'}, dimensions={2}, use_global_device_ids=true | all-gather | bytes 589824 | tf_op jit(solution)/shard_map/all_gather | solution.py:96
  141.9 3.8 %convolution_bitcast_fusion = f32[2,64,1024]{2,1,0:T(8,128)} fusion(bf16[2,16,64,128]{3,2,1,0:T(8,128)(2,1)S(1)} %all_gather.6, bf16[16,128,1024,1]{2,1,0,3:T(8,128)(2,1)} %bitcast.116), kind=kOutput, calls=%fused_computation.49 | convolution fusion | flops 536870912 | bytes 5242880 | tf_op jit(solution)/shard_map/bhnd,hdc->bnc/dot_general | solution.py:94
  145.7 0.0 all-reduce.4.cloned.1.call-update
  145.7 0.0 all-gather.2.cloned.1.call-start
  145.8 31.3 %all-reduce.4.cloned.1.call-done = f32[2,64,1024]{2,1,0:T(8,128)} async-done(((f32[2,64,1024]{2,1,0:T(8,128)}), f32[2,64,1024]{2,1,0:T(8,128)}) %all-reduce.4.cloned.1.call-update) | async-done | bytes 524304 | tf_op jit(solution)/shard_map/psum | solution.py:101
  177.1 1.2 multiply_reduce_fusion
  178.3 21.4 %psum.29 = f32[2,64]{1,0:T(2,128)S(1)} all-reduce(f32[2,64]{1,0:T(2,128)S(1)} %multiply_reduce_fusion), channel_id=1, replica_groups=mesh['seq'=8,'head'=4] {'seq'}, use_global_device_ids=true, to_apply=%region_11.12 | all-reduce | flops 128 | bytes 1024 | tf_op jit(solution)/shard_map/psum | solution.py:104
  199.7 1.9 multiply_convert_fusion
  201.5 0.0 all-gather.2.cloned.1.call-update
  201.6 0.1 reshape.135
  201.7 45.5 %all-gather.2.cloned.1.call-done = bf16[2,64,8192]{2,1,0:T(8,128)(2,1)} async-done(((bf16[2,64,1024]{2,1,0:T(8,128)(2,1)}), bf16[2,64,8192]{2,1,0:T(8,128)(2,1)}) %all-gather.2.cloned.1.call-update) | async-done | bytes 2097168 | tf_op jit(solution)/shard_map/all_gather | solution.py:108
  247.2 13.6 %fusion.44 = (f32[2,64]{1,0:T(2,128)S(1)}, f32[2,64,2048]{2,1,0:T(8,128)S(1)}) fusion(bf16[2,64,8192]{2,1,0:T(8,128)(2,1)} %all-gather.2.cloned.1.call-done, bf16[8192,2048]{1,0:T(8,128)(2,1)} %param.27), kind=kOutput, calls=%fused_computation.89 | convolution fusion | flops 4295229440 | bytes 36700672 | tf_op jit(solution)/shard_map/dot_general | solution.py:110
  260.8 0.7 gather_fusion
  261.6 0.1 broadcast_select_fusion
  261.7 0.7 copy.26
  262.4 39.2 %pmax.15 = f32[2,64]{1,0:T(2,128)S(1)} all-reduce(f32[2,64]{1,0:T(2,128)S(1)} %get-tuple-element.201), channel_id=1, replica_groups=mesh['seq'=8,'head'=4] {'seq','head'}, use_global_device_ids=true, to_apply=%region_15.16 | all-reduce | flops 128 | bytes 1024 | tf_op jit(solution)/shard_map/pmax | solution.py:116
  301.5 0.4 exponential_reduce_fusion
  301.9 40.0 %all-reduce.1 = (f32[2,64]{1,0:T(2,128)S(1)}, f32[2,64]{1,0:T(2,128)S(1)}) all-reduce(f32[2,64]{1,0:T(2,128)S(1)} %get-tuple-element.162, f32[2,64]{1,0:T(2,128)S(1)} %get-tuple-element.161), channel_id=1, replica_groups=mesh['seq'=8,'head'=4] {'seq','head'}, use_global_device_ids=true, to_apply=%region_13.14 | all-reduce | flops 256 | bytes 2048 | tf_op jit(solution)/shard_map/psum | solution.py:118
  341.9 0.6 add_subtract_fusion
  (34 shorter events, 0.3 us)
Async XLA Ops:
  7.2 106.6 %reduce-scatter.2.cloned.1.call-start = ((), (), s32[]{:S(2)}) async-start(), calls=%async_computation.1 | async-start | bytes 1179648 | tf_op jit(solution)/shard_map/reduce_scatter | solution.py:90
  9.1 42.7 %copy-start.6 = (u32[32]{0:T(128)S(1)}, u32[32]{0:T(128)}, u32[]{:S(2)}) copy-start(u32[32]{0:T(128)} %constant.93) | copy-start | bytes 388
  13.3 3.2 copy-start.1
  13.3 3.5 %copy-start.5 = (bf16[2,2,1024,128]{3,2,1,0:T(8,128)(2,1)S(1)}, bf16[2,2,1024,128]{3,2,1,0:T(8,128)(2,1)}, u32[]{:S(2)}) copy-start(bf16[2,2,1024,128]{3,2,1,0:T(8,128)(2,1)} %get-tuple-element.336) | copy-start | bytes 3145732 | tf_op jit(solution)/shard_map/while
  22.1 3.2 copy-start.1
  22.1 3.5 %copy-start.5 = (bf16[2,2,1024,128]{3,2,1,0:T(8,128)(2,1)S(1)}, bf16[2,2,1024,128]{3,2,1,0:T(8,128)(2,1)}, u32[]{:S(2)}) copy-start(bf16[2,2,1024,128]{3,2,1,0:T(8,128)(2,1)} %get-tuple-element.336) | copy-start | bytes 3145732 | tf_op jit(solution)/shard_map/while
  51.5 125.6 %all-reduce.4.cloned.1.call-start = ((), (), s32[]{:S(2)}) async-start(), calls=%async_computation.2 | async-start | bytes 1048576 | tf_op jit(solution)/shard_map/psum | solution.py:101
  86.4 59.3 %copy-start.2 = (bf16[1024]{0:T(1024)(128)(2,1)S(1)}, bf16[1024]{0:T(1024)(128)(2,1)}, u32[]{:S(2)}) copy-start(bf16[1024]{0:T(1024)(128)(2,1)} %param.26) | copy-start | bytes 6148
  86.4 90.7 %copy-start = (bf16[2,64,1024]{2,1,0:T(8,128)(2,1)S(1)}, bf16[2,64,1024]{2,1,0:T(8,128)(2,1)}, u32[]{:S(2)}) copy-start(bf16[2,64,1024]{2,1,0:T(8,128)(2,1)} %param.24) | copy-start | bytes 786436
  141.9 59.7 %copy-start.3 = (s32[2,6]{1,0:T(2,128)S(1)}, s32[2,6]{1,0:T(2,128)}, u32[]{:S(2)}) copy-start(s32[2,6]{1,0:T(2,128)} %param.21) | copy-start | bytes 148
  145.7 101.5 %all-gather.2.cloned.1.call-start = ((), (), s32[]{:S(2)}) async-start(), calls=%async_computation.3 | async-start | bytes 2359296 | tf_op jit(solution)/shard_map/all_gather | solution.py:108
  201.7 99.9 %copy-start.4 = (s32[2,64]{1,0:T(2,128)S(1)}, s32[2,64]{1,0:T(2,128)}, u32[]{:S(2)}) copy-start(s32[2,64]{1,0:T(2,128)} %param.23) | copy-start | bytes 1540
Sparse Core Ops, SparseCore 0:
  51.6 62.0 reduce-scatter.1
  145.8 31.2 all-reduce.3
  201.7 45.4 all-gather.1
where the time goes:
time: 350 us; the launch traced here: 349 us
  blocking collectives  184 us (53%)
  waiting for transfers between devices  104 us (30%)
  matrix products  27.8 us (8%)
  between operations  14.6 us (4%)
  other arithmetic  10.2 us (3%)
  local copies, waits for them, and re-layouts  7.47 us (2%)
    all_gather x1, waiting for transfers between devices, on_device(): portion = lax.all_gather(normed, 'seq', axis=2, tiled=True)  45.5 us
    psum x1, blocking collectives, on_device(): exp_sums, picked = lax.psum((local_sum, picked), ('seq', 'head'))  40 us
    pmax x1, blocking collectives, on_device(): vocab_top = lax.pmax(local_max, ('seq', 'head'))  39.2 us
    unnamed x1, blocking collectives  33.4 us
    psum x1, waiting for transfers between devices, on_device(): projected = lax.psum(projected, 'head')  31.3 us
    reduce_scatter x1, waiting for transfers between devices, on_device(): lax.psum_scatter(scaled, 'seq', scatter_dimension=2, tiled=True)  27.2 us
    all_gather x1, blocking collectives, on_device(): lax.all_gather(attention, 'seq', axis=2, tiled=True)  27.1 us
    pmax x1, blocking collectives, on_device(): highest = lax.pmax(maxima, 'seq')  23.4 us
  transfers between devices with their start and end apart: 3, of which 3 were waited for; matrix products, arithmetic and copies ran while one was open for 0% of the time, Pallas kernels for 0%

commit v1 on v0

--- a/solution.py
+++ b/solution.py
@@ -98,7 +98,11 @@
         preferred_element_type=jnp.float32,
     )
     vocab_local = vocab_weight.shape[1]
-    projected = lax.psum(projected, "head")
+    projected = projected
+    for hop in (1, 2):
+        projected = projected + lax.ppermute(
+            projected, "head", [(dev, dev ^ hop) for dev in range(4)]
+        )
     stream = residual.astype(jnp.float32) + projected
     gain_part = norm_gain.astype(jnp.float32)
     square_sum = lax.psum(jnp.sum(stream * stream, axis=-1), "seq")

time: 350 us -> 330 us (0.943)
  waiting for transfers between devices: 104 us -> 88.2 us
    psum x1 -> x0, waiting for transfers between devices: 31.3 us -> none  [on_device(): projected = lax.psum(projected, 'head')]
    ppermute x0 -> x2, waiting for transfers between devices: none -> 14.3 us  [on_device(): lax.ppermute(projected, 'head', [(dev, dev ^ hop) for dev in range(4)])]
  transfers between devices with their start and end apart: 3 -> 4, of which waited for: 3 -> 4; matrix products, arithmetic and copies ran while one was open for 0% -> 0% of each run, Pallas kernels for 0% -> 0%
where the time goes in v1:
time: 330 us; the launch traced here: 329 us
  blocking collectives  181 us (55%)
  waiting for transfers between devices  88.2 us (27%)
  matrix products  27 us (8%)
  between operations  14.9 us (5%)
  other arithmetic  8.25 us (2%)
  local copies, waits for them, and re-layouts  7.46 us (2%)
    all_gather x1, waiting for transfers between devices, on_device(): portion = lax.all_gather(normed, 'seq', axis=2, tiled=True)  46.7 us
    psum x1, blocking collectives, on_device(): exp_sums, picked = lax.psum((local_sum, picked), ('seq', 'head'))  40 us
    pmax x1, blocking collectives, on_device(): vocab_top = lax.pmax(local_max, ('seq', 'head'))  39.2 us
    unnamed x1, blocking collectives  33.4 us
    reduce_scatter x1, waiting for transfers between devices, on_device(): lax.psum_scatter(scaled, 'seq', scatter_dimension=2, tiled=True)  27.2 us
    all_gather x1, blocking collectives, on_device(): lax.all_gather(attention, 'seq', axis=2, tiled=True)  27.2 us
    pmax x1, blocking collectives, on_device(): highest = lax.pmax(maxima, 'seq')  23.4 us
    psum x1, blocking collectives, on_device(): square_sum = lax.psum(jnp.sum(stream * stream, axis=-1), 'seq')  18.3 us
  transfers between devices with their start and end apart: 4, of which 4 were waited for; matrix products, arithmetic and copies ran while one was open for 0% of the time, Pallas kernels for 0%

profile of v1, /device:TPU:0, one launch (start us, length us, event | category | flops | bytes accessed | tf_op | source)
XLA Modules:
  0.0 329.1 jit_solution(9262301445488805071)
XLA Ops:
  7.2 0.0 reduce-scatter.2.cloned.1.call-start
  7.3 1.0 convolution_minimum_fusion.6
  8.2 0.3 convolution_minimum_fusion.4
  8.5 0.3 convolution_minimum_fusion.2
  8.8 0.3 fusion.30
  9.1 0.0 copy-start.6
  9.1 17.6 %while.15 = (s32[]{:T(128)}, f32[2,2,512]{2,1,0:T(2,128)S(1)}, f32[2,2,512]{2,1,0:T(2,128)S(1)}, f32[2,2,512,128]{3,2,1,0:T(8,128)S(1)}, s32[2]{0:T(128)}, /*ind...) while((s32[]{:T(128)}, f32[2,2,512]{2,1,0:T(2,128)S(1)}, ...), condition=%wide.region_5.6_spmd.clone, body=%wide.region_0.5_spmd.clone.sunk | while | flops 587279360 | bytes 21873904 | solution.py:81
  9.1 1.0 constant_dynamic-slice_fusion.5
  10.1 0.1 copy.30
  10.3 0.2 and.42
  10.4 1.0 fusion.69
  11.4 0.1 convert_reduce_fusion.4
  11.5 1.2 dynamic_slice.68
  12.7 0.6 add_compare_fusion.2
  13.3 0.0 copy-start.1
  13.3 0.0 copy-start.5
  13.3 2.0 fusion.70
  15.3 1.2 convert_reduce_fusion.5
  16.5 0.3 convolution_multiply_fusion.4
  16.9 1.0 fusion.73
  17.9 1.0 constant_dynamic-slice_fusion.5
  18.9 0.1 copy.30
  19.1 0.2 and.42
  19.2 1.0 fusion.69
  20.2 0.1 convert_reduce_fusion.4
  20.3 1.2 dynamic_slice.68
  21.5 0.6 add_compare_fusion.2
  22.1 0.0 copy-start.1
  22.1 2.0 fusion.70
  24.1 1.2 convert_reduce_fusion.5
  25.3 0.3 convolution_multiply_fusion.4
  25.7 1.0 fusion.73
  26.7 23.4 %pmax.14 = f32[2,2,512]{2,1,0:T(2,128)S(1)} all-reduce(f32[2,2,512]{2,1,0:T(2,128)S(1)} %get-tuple-element.72), channel_id=1, replica_groups=mesh['seq'=8,'head'=4] {'seq'}, use_global_device_ids=true, to_apply=%region_6.7 | all-reduce | flops 2048 | bytes 16384 | tf_op jit(solution)/shard_map/pmax | solution.py:85
  50.2 1.3 broadcast_multiply_fusion
  51.5 0.0 reduce-scatter.2.cloned.1.call-update
  51.5 0.0 all-gather.2.cloned.1.call-start
  51.6 0.1 reshape.133
  51.7 0.1 copy.24
  51.8 0.6 dynamic-slice
  53.0 33.4 %all-reduce = f32[2,16,64]{1,0,2:T(2,128)S(1)} all-reduce(f32[2,16,64]{1,0,2:T(2,128)S(1)} %copy.24), channel_id=3, replica_groups=mesh['seq'=8,'head'=4] {'seq'}, use_global_device_ids=true, to_apply=%region_8.9.clone | all-reduce | flops 2048 | bytes 16384
  86.5 0.1 copy.25
  86.5 27.2 %reduce-scatter.2.cloned.1.call-done = f32[2,16,8,128]{3,2,1,0:T(8,128)} async-done(((f32[2,16,64,128]{3,2,1,0:T(8,128)}), f32[2,16,8,128]{3,2,1,0:T(8,128)}) %reduce-scatter.2.cloned.1.call-update) | async-done | bytes 131088 | tf_op jit(solution)/shard_map/reduce_scatter | solution.py:90
  113.7 1.0 divide_convert_fusion
  114.7 27.2 %all_gather.6 = bf16[2,16,64,128]{3,2,1,0:T(8,128)(2,1)S(1)} all-gather(bf16[2,16,8,128]{3,2,1,0:T(8,128)(2,1)S(1)} %divide_convert_fusion), channel_id=1, replica_groups=mesh['seq'=8,'head'=4] {'seq'}, dimensions={2}, use_global_device_ids=true | all-gather | bytes 589824 | tf_op jit(solution)/shard_map/all_gather | solution.py:96
  141.9 2.9 convolution_bitcast_fusion
  144.9 0.1 collective-permute-start
  144.9 1.9 collective-permute-done
  146.8 0.1 add.71
  146.9 1.6 collective-permute-start.1
  148.5 12.4 %collective-permute-done.1 = f32[2,64,1024]{2,1,0:T(8,128)S(1)} collective-permute-done((f32[2,64,1024]{2,1,0:T(8,128)S(1)}, f32[2,64,1024]{2,1,0:T(8,128)S(1)}, u32[]{:S(2)}, u32[]{:S(2)}) %collective-permute-start.1) | collective-permute-done | bytes 524320 | tf_op jit(solution)/shard_map/ppermute | solution.py:103
  160.9 0.2 multiply_reduce_fusion
  161.1 18.3 %psum.21 = f32[2,64]{1,0:T(2,128)S(1)} all-reduce(f32[2,64]{1,0:T(2,128)S(1)} %multiply_reduce_fusion), channel_id=1, replica_groups=mesh['seq'=8,'head'=4] {'seq'}, use_global_device_ids=true, to_apply=%region_10.11 | all-reduce | flops 128 | bytes 1024 | tf_op jit(solution)/shard_map/psum | solution.py:108
  179.4 0.8 multiply_convert_fusion
  180.2 0.0 all-gather.2.cloned.1.call-update
  180.3 0.1 reshape.135
  180.4 46.7 %all-gather.2.cloned.1.call-done = bf16[2,64,8192]{2,1,0:T(8,128)(2,1)} async-done(((bf16[2,64,1024]{2,1,0:T(8,128)(2,1)}), bf16[2,64,8192]{2,1,0:T(8,128)(2,1)}) %all-gather.2.cloned.1.call-update) | async-done | bytes 2097168 | tf_op jit(solution)/shard_map/all_gather | solution.py:112
  227.1 13.6 %fusion.44 = (f32[2,64]{1,0:T(2,128)S(1)}, f32[2,64,2048]{2,1,0:T(8,128)S(1)}) fusion(bf16[2,64,8192]{2,1,0:T(8,128)(2,1)} %all-gather.2.cloned.1.call-done, bf16[8192,2048]{1,0:T(8,128)(2,1)} %param.27), kind=kOutput, calls=%fused_computation.89 | convolution fusion | flops 4295229440 | bytes 36700672 | tf_op jit(solution)/shard_map/dot_general | solution.py:114
  240.6 0.7 gather_fusion
  241.4 0.1 broadcast_select_fusion
  241.5 0.7 copy.26
  242.2 39.2 %pmax.15 = f32[2,64]{1,0:T(2,128)S(1)} all-reduce(f32[2,64]{1,0:T(2,128)S(1)} %get-tuple-element.201), channel_id=1, replica_groups=mesh['seq'=8,'head'=4] {'seq','head'}, use_global_device_ids=true, to_apply=%region_14.15 | all-reduce | flops 128 | bytes 1024 | tf_op jit(solution)/shard_map/pmax | solution.py:120
  281.4 0.4 exponential_reduce_fusion
  281.8 40.0 %all-reduce.1 = (f32[2,64]{1,0:T(2,128)S(1)}, f32[2,64]{1,0:T(2,128)S(1)}) all-reduce(f32[2,64]{1,0:T(2,128)S(1)} %get-tuple-element.162, f32[2,64]{1,0:T(2,128)S(1)} %get-tuple-element.161), channel_id=1, replica_groups=mesh['seq'=8,'head'=4] {'seq','head'}, use_global_device_ids=true, to_apply=%region_12.13 | all-reduce | flops 256 | bytes 2048 | tf_op jit(solution)/shard_map/psum | solution.py:122
  321.7 0.6 add_subtract_fusion
  (36 shorter events, 0.3 us)
Async XLA Ops:
  7.2 106.6 %reduce-scatter.2.cloned.1.call-start = ((), (), s32[]{:S(2)}) async-start(), calls=%async_computation.1 | async-start | bytes 1179648 | tf_op jit(solution)/shard_map/reduce_scatter | solution.py:90
  9.1 42.7 %copy-start.6 = (u32[32]{0:T(128)S(1)}, u32[32]{0:T(128)}, u32[]{:S(2)}) copy-start(u32[32]{0:T(128)} %constant.93) | copy-start | bytes 388
  13.3 3.2 copy-start.1
  13.3 3.5 %copy-start.5 = (bf16[2,2,1024,128]{3,2,1,0:T(8,128)(2,1)S(1)}, bf16[2,2,1024,128]{3,2,1,0:T(8,128)(2,1)}, u32[]{:S(2)}) copy-start(bf16[2,2,1024,128]{3,2,1,0:T(8,128)(2,1)} %get-tuple-element.336) | copy-start | bytes 3145732 | tf_op jit(solution)/shard_map/while
  22.1 3.2 copy-start.1
  22.1 3.5 %copy-start.5 = (bf16[2,2,1024,128]{3,2,1,0:T(8,128)(2,1)S(1)}, bf16[2,2,1024,128]{3,2,1,0:T(8,128)(2,1)}, u32[]{:S(2)}) copy-start(bf16[2,2,1024,128]{3,2,1,0:T(8,128)(2,1)} %get-tuple-element.336) | copy-start | bytes 3145732 | tf_op jit(solution)/shard_map/while
  51.5 175.5 %all-gather.2.cloned.1.call-start = ((), (), s32[]{:S(2)}) async-start(), calls=%async_computation.2 | async-start | bytes 2359296 | tf_op jit(solution)/shard_map/all_gather | solution.py:112
  141.9 6.6 %copy-start.2 = (bf16[1024]{0:T(1024)(128)(2,1)S(1)}, bf16[1024]{0:T(1024)(128)(2,1)}, u32[]{:S(2)}) copy-start(bf16[1024]{0:T(1024)(128)(2,1)} %param.26) | copy-start | bytes 6148
  141.9 19.0 %copy-start = (bf16[2,64,1024]{2,1,0:T(8,128)(2,1)S(1)}, bf16[2,64,1024]{2,1,0:T(8,128)(2,1)}, u32[]{:S(2)}) copy-start(bf16[2,64,1024]{2,1,0:T(8,128)(2,1)} %param.24) | copy-start | bytes 786436
  141.9 38.4 %copy-start.3 = (s32[2,6]{1,0:T(2,128)S(1)}, s32[2,6]{1,0:T(2,128)}, u32[]{:S(2)}) copy-start(s32[2,6]{1,0:T(2,128)} %param.21) | copy-start | bytes 148
  144.9 2.0 collective-permute-start
  146.9 14.0 %collective-permute-start.1 = (f32[2,64,1024]{2,1,0:T(8,128)S(1)}, f32[2,64,1024]{2,1,0:T(8,128)S(1)}, u32[]{:S(2)}, u32[]{:S(2)}) collective-permute-start(f32[2,64,1024]{2,1,0:T(8,128)S(1)} %add.71), channel_id=1, source_target_pairs={{0,2},{1,3},{2,0},{3,1},{4,6},{5,7},{6,4},{7,5},{8,10},{9,11},{10,... | collective-permute-start | bytes 1572872 | tf_op jit(solution)/shard_map/ppermute | solution.py:103
  180.4 101.0 %copy-start.4 = (s32[2,64]{1,0:T(2,128)S(1)}, s32[2,64]{1,0:T(2,128)}, u32[]{:S(2)}) copy-start(s32[2,64]{1,0:T(2,128)} %param.23) | copy-start | bytes 1540
Sparse Core Ops, SparseCore 0:
  51.6 62.0 reduce-scatter.1
  180.4 46.6 all-gather.1
